TPU v7x, 256 devices: a whole 4x4x8 slice. The times are simulated.
256 devices in a mesh: section: 2 (over y_hi), sx: 16 (over z, core), sy: 8 (over y_lo, x).
Axes of the slice: x: 4, y: 4 (y_hi: 2, y_lo: 2; y = y_hi * 2 + y_lo), z: 8, core: 2. Of those that a mesh axis runs over, the one named last changes fastest.
Arguments:
- previous: float32 [16, 256, 1024], P(None, 'sx', 'sy'), may hold values from -3 to 3
- sections: float32 [4, 16, 256, 1024], P('section', None, 'sx', 'sy'), may hold values from -3 to 3
- diffusivity: float32 [16, 256, 1024], P(None, 'sx', 'sy'), may hold values from 0.3 to 3
- reaction: float32 [16, 256, 1024], P(None, 'sx', 'sy'), may hold values from 0.2 to 2
Outputs:
- updated: float32 [4, 16, 256, 1024], P('section', None, 'sx', 'sy')
All inputs are finite; a program needn't handle non-finite values.
Results may differ from a plain program's by a relative error of at most 0.0003.
Values sent between devices are 32-bit elements; how exact they have to be, the bound alone decides.
No kernel may reach another device: no remote copies, remote signals or barrier semaphores. Data moves between devices by JAX's collectives and lax.ppermute only.
A program may use at most 64 MiB of HBM per device.

v0:
```python
import jax
import jax.numpy as jnp
from jax import lax
from jax.sharding import PartitionSpec as P

ITERS = 4
step_size = 1.0
tiny_value = 1e-06


def extended(cells, sides, width):
    for axis, dim in sides:
        count = lax.axis_size(axis)
        ends = count - 1
        head = lax.slice_in_dim(cells, 0, width, axis=dim)
        tail = lax.slice_in_dim(cells, cells.shape[dim] - width, cells.shape[dim], axis=dim)
        cells = jnp.concatenate(
            [
                lax.ppermute(tail, axis, [(i, (i + 1) % count) for i in range(ends)]),
                cells,
                lax.ppermute(head, axis, [((i + 1) % count, i) for i in range(ends)]),
            ],
            axis=dim,
        )
    return cells


def invert_table(matrix):
    order_n = len(matrix)
    augmented = [
        list(matrix[r]) + [1.0 if c == r else 0.0 for c in range(order_n)] for r in range(order_n)
    ]
    for col in range(order_n):
        pivot_row = max(range(col, order_n), key=lambda r: abs(augmented[r][col]))
        augmented[col], augmented[pivot_row] = (augmented[pivot_row], augmented[col])
        leading = augmented[col][col]
        augmented[col] = [v / leading for v in augmented[col]]
        for r in range(order_n):
            if r != col:
                factor = augmented[r][col]
                augmented[r] = [a - factor * b for a, b in zip(augmented[r], augmented[col])]
    return [row_values[order_n:] for row_values in augmented]


def table_product(left, right):
    return [
        [sum((left[i][k] * right[k][j] for k in range(len(right)))) for j in range(len(right[0]))]
        for i in range(len(left))
    ]


def pair_add(first, second):
    return (first[0] + second[0], first[1] + second[1])


def pair_sub(first, second):
    return (first[0] - second[0], first[1] - second[1])


def pair_mul(first, second):
    return (
        first[0] * second[0] - first[1] * second[1],
        first[0] * second[1] + first[1] * second[0],
    )


def pair_div(first, second):
    scale_sq = second[0] * second[0] + second[1] * second[1]
    return (
        (first[0] * second[0] + first[1] * second[1]) / scale_sq,
        (first[1] * second[0] - first[0] * second[1]) / scale_sq,
    )


def quartic_value(point):
    return (((210.0 * point - 480.0) * point + 360.0) * point - 96.0) * point + 6.0


def bisect_root(lower, upper):
    for count in range(200):
        middle = 0.5 * (lower + upper)
        if (quartic_value(lower) < 0.0) == (quartic_value(middle) < 0.0):
            lower = middle
        else:
            upper = middle
    return 0.5 * (lower + upper)


def radau_tables():
    abscissae = []
    grid_steps = 4000
    for m in range(grid_steps):
        lower = 0.999 * m / grid_steps
        upper = 0.999 * (m + 1) / grid_steps
        if (quartic_value(lower) < 0.0) != (quartic_value(upper) < 0.0):
            abscissae.append(bisect_root(lower, upper))
    abscissae.append(1.0)
    vander = [[abscissae[j] ** k for k in range(4)] for j in range(4)]
    moments = [[abscissae[i] ** (k + 1) / (k + 1) for k in range(4)] for i in range(4)]
    tableau = table_product(moments, invert_table(vander))
    inverse = invert_table(tableau)
    running = [list(row_values) for row_values in inverse]
    coeffs = []
    for k in range(1, 5):
        trace_value = sum((running[i][i] for i in range(4)))
        coeffs.append(-trace_value / k)
        shifted_table = [
            [running[i][j] + (coeffs[-1] if i == j else 0.0) for j in range(4)] for i in range(4)
        ]
        running = table_product(inverse, shifted_table)
    start_point = (0.4, 0.9)
    estimates = [(1.0, 0.0)]
    for k in range(3):
        estimates.append(pair_mul(estimates[-1], start_point))
    for count in range(500):
        for i in range(4):
            value = (1.0, 0.0)
            for coef_value in coeffs:
                value = pair_add(pair_mul(value, estimates[i]), (coef_value, 0.0))
            denom = (1.0, 0.0)
            for j in range(4):
                if j != i:
                    denom = pair_mul(denom, pair_sub(estimates[i], estimates[j]))
            estimates[i] = pair_sub(estimates[i], pair_div(value, denom))
    chosen = [m for m in range(4) if estimates[m][1] > 0.0]
    ranking = sorted(chosen, key=lambda m: -estimates[m][1])
    columns = []
    pairs = []
    for m in ranking:
        eigen_pair = estimates[m]
        system = [
            [
                (
                    inverse[i][j] - (eigen_pair[0] if i == j else 0.0),
                    -(eigen_pair[1] if i == j else 0.0),
                )
                for j in range(4)
            ]
            for i in range(3)
        ]
        rows_left = [
            [system[i][j] for j in range(3)] + [(-system[i][3][0], -system[i][3][1])]
            for i in range(3)
        ]
        for col in range(3):
            pivot_row = max(
                range(col, 3), key=lambda r: rows_left[r][col][0] ** 2 + rows_left[r][col][1] ** 2
            )
            rows_left[col], rows_left[pivot_row] = (rows_left[pivot_row], rows_left[col])
            leading = rows_left[col][col]
            rows_left[col] = [pair_div(v, leading) for v in rows_left[col]]
            for r in range(3):
                if r != col:
                    factor = rows_left[r][col]
                    rows_left[r] = [
                        pair_sub(a, pair_mul(factor, b))
                        for a, b in zip(rows_left[r], rows_left[col])
                    ]
        vector = [rows_left[i][3] for i in range(3)] + [(1.0, 0.0)]
        columns.append([v[0] for v in vector])
        columns.append([v[1] for v in vector])
        pairs.append((eigen_pair[0], eigen_pair[1]))
    eigen_basis = [[columns[j][i] for j in range(4)] for i in range(4)]
    basis_inverse = invert_table(eigen_basis)
    return (tableau, inverse, eigen_basis, basis_inverse, pairs)


def center(padded):
    return padded[..., 1:-1, 1:-1, 1:-1]


def shifted(padded, member):
    if member == 0:
        return padded[..., 2:, 1:-1, 1:-1]
    if member == 1:
        return padded[..., :-2, 1:-1, 1:-1]
    if member == 2:
        return padded[..., 1:-1, 2:, 1:-1]
    if member == 3:
        return padded[..., 1:-1, :-2, 1:-1]
    if member == 4:
        return padded[..., 1:-1, 1:-1, 2:]
    return padded[..., 1:-1, 1:-1, :-2]


def face_terms(padded):
    middle = center(padded)
    return [0.5 * (middle + shifted(padded, m)) for m in range(6)]


def face_total(faces):
    total = faces[0]
    for m in range(1, 6):
        total = total + faces[m]
    return total


def neighbour_sum(faces, padded):
    total = faces[0] * shifted(padded, 0)
    for m in range(1, 6):
        total = total + faces[m] * shifted(padded, m)
    return total


def pad_depth(field, width):
    return jnp.pad(field, [(0, 0)] * (field.ndim - 3) + [(width, width), (0, 0), (0, 0)])


def trim_cells(field, width):
    if width == 0:
        return field
    return field[..., width:-width, width:-width, width:-width]


def apply_inverse(diag_real, coupling, determinant, vector):
    first = (diag_real * vector[0] - coupling * vector[1]) / determinant
    second = (coupling * vector[0] + diag_real * vector[1]) / determinant
    return jnp.stack([first, second])


def apply_block(diag_real, coupling, vector):
    return jnp.stack(
        [diag_real * vector[0] + coupling * vector[1], diag_real * vector[1] - coupling * vector[0]]
    )


def combine(coef, fields):
    total = coef[:, 0][:, None, None, None] * fields[0][None]
    for column in range(1, fields.shape[0]):
        total = total + coef[:, column][:, None, None, None] * fields[column][None]
    return total


def body(previous, sections, diffusivity, reaction):
    tableau, inverse, eigen_basis, basis_inverse, pairs = radau_tables()
    flux_rows = jnp.asarray(basis_inverse, jnp.float32)
    shift_table = table_product(basis_inverse, inverse)
    shift_rows = jnp.asarray(
        [[v / step_size for v in row_values] for row_values in shift_table], jnp.float32
    )
    basis_rows = jnp.asarray(eigen_basis, jnp.float32)
    pair_table = jnp.asarray([list(p) for p in pairs], jnp.float32)
    eigen_block = lax.axis_index("section")
    section_coef = diffusivity * (1.0 + 0.5 * jnp.tanh(sections))
    frozen_coef = diffusivity * (1.0 + 0.5 * jnp.tanh(previous))
    react_slope = reaction * (1.0 - 3.0 * previous * previous)
    coefs = jnp.concatenate([section_coef, frozen_coef[None], react_slope[None]], 0)
    halo_width = 1
    section_pad, coef_pad = (
        extended(sections, (("sx", 2), ("sy", 3)), halo_width),
        extended(coefs, (("sx", 2), ("sy", 3)), halo_width),
    )
    section_pad = pad_depth(section_pad, halo_width)
    coef_pad = pad_depth(coef_pad, halo_width)
    section_near = trim_cells(section_pad, halo_width - 1)
    coef_near = trim_cells(coef_pad, halo_width - 1)
    section_faces = face_terms(coef_near[:2])
    section_flux = neighbour_sum(section_faces, section_near) - face_total(section_faces) * sections
    section_flux = section_flux + reaction * sections * (1.0 - sections * sections)
    increment = sections - previous
    all_flux, all_increment = (
        lax.all_gather(section_flux, "section", axis=0, tiled=True),
        lax.all_gather(increment, "section", axis=0, tiled=True),
    )
    own_flux = lax.dynamic_slice(flux_rows, (2 * eigen_block, 0), (2, 4))
    own_shift = lax.dynamic_slice(shift_rows, (2 * eigen_block, 0), (2, 4))
    rhs = combine(own_flux, all_flux) - combine(own_shift, all_increment)
    faces_region = face_terms(coef_pad[2])
    slope_region = trim_cells(coef_pad[3], 1)
    real_part = pair_table[eigen_block, 0] / step_size
    coupling = pair_table[eigen_block, 1] / step_size
    diag_region = real_part + face_total(faces_region) - slope_region
    det_region = diag_region * diag_region + coupling * coupling
    inner_cut = halo_width - 1
    faces_inner = [trim_cells(face, inner_cut) for face in faces_region]
    diag_inner = trim_cells(diag_region, inner_cut)
    det_inner = trim_cells(det_region, inner_cut)
    residue = rhs
    correction = jnp.zeros_like(residue)
    for sweep in range(ITERS):
        scaled = apply_inverse(diag_inner, coupling, det_inner, residue)
        scaled_pad = extended(scaled, (("sx", 2), ("sy", 3)), halo_width)
        scaled_pad = pad_depth(scaled_pad, halo_width)
        search = scaled + apply_inverse(
            diag_inner, coupling, det_inner, neighbour_sum(faces_inner, scaled_pad)
        )
        search_pad = extended(search, (("sx", 2), ("sy", 3)), 1)
        search_pad = pad_depth(search_pad, 1)
        image = apply_block(diag_inner, coupling, search) - neighbour_sum(faces_inner, search_pad)
        numerator, denominator = lax.psum(
            (jnp.sum(image * residue), jnp.sum(image * image)), ("sx", "sy")
        )
        step_length = numerator / (denominator + tiny_value)
        correction = correction + step_length * search
        residue = residue - step_length * image
    gathered = lax.all_gather(correction, "section", axis=0, tiled=True)
    own_basis = lax.dynamic_slice(basis_rows, (2 * eigen_block, 0), (2, 4))
    return sections + combine(own_basis, gathered)


def solution(mesh):
    in_specs = (
        P(None, "sx", "sy"),
        P("section", None, "sx", "sy"),
        P(None, "sx", "sy"),
        P(None, "sx", "sy"),
    )
    out_specs = P("section", None, "sx", "sy")
    return jax.shard_map(body, mesh=mesh, in_specs=in_specs, out_specs=out_specs, check_vma=False)
```

profile of v0, /device:TPU:130, one launch (start us, length us, event | category | flops | bytes accessed | tf_op | source)
XLA Modules:
  0.0 1369.5 jit_solution(1758878238142489170)
XLA Ops:
  3.7 4.9 collective-permute-start.5
  10.4 8.7 all_gather.10
  26.2 4.9 collective-permute-start.1
  52.7 8.6 all_gather.9
  66.1 4.9 collective-permute-start.9
  72.6 4.7 collective-permute-start.10
  82.4 6.5 collective-permute-done.11
  92.5 4.9 collective-permute-start.13
  109.4 4.3 collective-permute-done.15
  116.1 276.0 %all-reduce.13 = (f32[]{:T(128)}, f32[]{:T(128)}) all-reduce(f32[]{:T(128)} %get-tuple-element.12, f32[]{:T(128)} %get-tuple-element.11), channel_id=1, replica_groups=mesh['section'=2,'sx'=16,'sy'=8] {'sx','sy'}, use_global_device_ids=true, to_apply=%region_1.2 | all-reduce | flops 2 | bytes 16 | tf_op jit(solution)/shard_map/psum | solution.py:290
  397.2 4.9 collective-permute-start.17
  417.8 4.9 collective-permute-start.21
  426.2 4.1 collective-permute-start.23
  436.3 278.6 %all-reduce.12 = (f32[]{:T(128)}, f32[]{:T(128)}) all-reduce(f32[]{:T(128)} %get-tuple-element.10, f32[]{:T(128)} %get-tuple-element.9), channel_id=1, replica_groups=mesh['section'=2,'sx'=16,'sy'=8] {'sx','sy'}, use_global_device_ids=true, to_apply=%region_5.6 | all-reduce | flops 2 | bytes 16 | tf_op jit(solution)/shard_map/psum | solution.py:290
  719.0 4.9 collective-permute-start.25
  727.3 3.9 collective-permute-start.27
  739.6 4.9 collective-permute-start.29
  758.1 278.6 %all-reduce.11 = (f32[]{:T(128)}, f32[]{:T(128)}) all-reduce(f32[]{:T(128)} %get-tuple-element.8, f32[]{:T(128)} %get-tuple-element.7), channel_id=1, replica_groups=mesh['section'=2,'sx'=16,'sy'=8] {'sx','sy'}, use_global_device_ids=true, to_apply=%region_9.10 | all-reduce | flops 2 | bytes 16 | tf_op jit(solution)/shard_map/psum | solution.py:290
  1040.7 4.9 collective-permute-start.33
  1049.1 3.9 collective-permute-start.35
  1061.3 4.9 collective-permute-start.37
  1069.7 3.9 collective-permute-start.39
  1079.8 278.7 %all-reduce.10 = (f32[]{:T(128)}, f32[]{:T(128)}) all-reduce(f32[]{:T(128)} %get-tuple-element.6, f32[]{:T(128)} %get-tuple-element.5), channel_id=1, replica_groups=mesh['section'=2,'sx'=16,'sy'=8] {'sx','sy'}, use_global_device_ids=true, to_apply=%region_13.14 | all-reduce | flops 2 | bytes 16 | tf_op jit(solution)/shard_map/psum | solution.py:290
  1360.0 8.6 all_gather.11
  (198 shorter events, 144.1 us)
Async XLA Ops:
  1.8 22.3 %collective-permute-start.4 = (f32[2,16,1,128]{3,1,2,0:T(8,128)S(1)}, f32[2,16,1,128]{3,1,2,0:T(8,128)S(1)}, u32[]{:S(2)}, u32[]{:S(2)}) collective-permute-start(f32[2,16,1,128]{3,1,2,0:T(8,128)S(1)} %get-tuple-element.109), channel_id=1, source_target_pairs={{0,8},{8,16},{16,24},{24,32},{32,40},{40,48},{48,56},{56,64},{64,7... | collective-permute-start | bytes 49160 | tf_op jit(solution)/shard_map/ppermute | solution.py:19
  3.7 27.3 %collective-permute-start.5 = (f32[2,16,1,128]{3,1,2,0:T(8,128)S(1)}, f32[2,16,1,128]{3,1,2,0:T(8,128)S(1)}, u32[]{:S(2)}, u32[]{:S(2)}) collective-permute-start(f32[2,16,1,128]{3,1,2,0:T(8,128)S(1)} %get-tuple-element.108), channel_id=1, source_target_pairs={{8,0},{16,8},{24,16},{32,24},{40,32},{48,40},{56,48},{64,56},{72,6... | collective-permute-start | bytes 49160 | tf_op jit(solution)/shard_map/ppermute | solution.py:21
  24.3 13.5 collective-permute-start
  26.2 11.6 collective-permute-start.1
  31.2 13.7 collective-permute-start.6
  34.6 10.3 collective-permute-start.7
  38.6 7.8 collective-permute-start.2
  72.6 9.8 collective-permute-start.10
  77.3 11.6 collective-permute-start.11
  99.0 10.4 collective-permute-start.14
  102.6 11.1 collective-permute-start.15
  403.6 8.6 collective-permute-start.18
  405.6 8.6 collective-permute-start.19
  424.2 8.6 collective-permute-start.22
  426.2 8.6 collective-permute-start.23
  725.4 8.6 collective-permute-start.26
  727.3 8.6 collective-permute-start.27
  746.0 8.6 collective-permute-start.30
  747.9 8.6 collective-permute-start.31
  1047.1 8.6 collective-permute-start.34
  1049.1 8.6 collective-permute-start.35
  1059.4 6.8 collective-permute-start.36
  1067.7 8.6 collective-permute-start.38
  1069.7 8.6 collective-permute-start.39
  (33 other events, 827.5 us)
where the time goes:
time: 1370 us
  blocking collectives  1140 us (83%)
  starting transfers between devices  128 us (9%)
  waiting for transfers between devices  55.5 us (4%)
  other arithmetic  29.6 us (2%)
    psum x4, blocking collectives, body(): lax.psum((jnp.sum(image * residue), jnp.sum(image * image)), ('sx', 'sy'))  1110 us
    ppermute x20, starting transfers between devices, extended(): lax.ppermute(head, axis, [((i + 1) % count, i) for i in range(ends)])  82.7 us
    ppermute x20, starting transfers between devices, extended(): lax.ppermute(tail, axis, [(i, (i + 1) % count) for i in range(ends)])  45.1 us
    ppermute x20, waiting for transfers between devices, extended(): lax.ppermute(head, axis, [((i + 1) % count, i) for i in range(ends)])  34.4 us
  transfers between devices with their start and end apart: 40, of which 25 were waited for; matrix products, arithmetic and copies ran while one was open for 1% of the time, Pallas kernels for 0%

commit v1 on v0

--- a/solution.py
+++ b/solution.py
@@ -6,6 +6,12 @@
 ITERS = 4
 step_size = 1.0
 tiny_value = 1e-06
+
+
+def edit_turns(shard_in):
+    for ii in ("sx", "sy"):
+        shard_in = lax.psum(shard_in, ii)
+    return shard_in
 
 
 def extended(cells, sides, width):
@@ -287,9 +293,7 @@
         search_pad = extended(search, (("sx", 2), ("sy", 3)), 1)
         search_pad = pad_depth(search_pad, 1)
         image = apply_block(diag_inner, coupling, search) - neighbour_sum(faces_inner, search_pad)
-        numerator, denominator = lax.psum(
-            (jnp.sum(image * residue), jnp.sum(image * image)), ("sx", "sy")
-        )
+        numerator, denominator = edit_turns((jnp.sum(image * residue), jnp.sum(image * image)))
         step_length = numerator / (denominator + tiny_value)
         correction = correction + step_length * search
         residue = residue - step_length * image

time: 1370 us -> 457 us (0.33)
  blocking collectives: 1140 us -> 195 us
  waiting for transfers between devices: 55.5 us -> 74.4 us
    psum x4 -> x8, blocking collectives: 1110 us -> 170 us  [edit_turns(): shard_in = lax.psum(shard_in, ii)]
    ppermute x20, waiting for transfers between devices: 34.4 us -> 54.5 us  [extended(): lax.ppermute(head, axis, [((i + 1) % count, i) for i in range(ends)])]
    ppermute x20, starting transfers between devices: 45.1 us -> 64.1 us  [extended(): lax.ppermute(tail, axis, [(i, (i + 1) % count) for i in range(ends)])]
  transfers between devices with their start and end apart: 40 -> 40, of which waited for: 25 -> 25; matrix products, arithmetic and copies ran while one was open for 1% -> 2% of each run, Pallas kernels for 0% -> 0%
where the time goes in v1:
time: 457 us; the launch traced here: 451 us
  blocking collectives  195 us (43%)
  starting transfers between devices  135 us (30%)
  waiting for transfers between devices  74.4 us (16%)
  other arithmetic  28 us (6%)
  local copies, waits for them, and re-layouts  11 us (2%)
  between operations  7.25 us (2%)
    psum x8, blocking collectives, edit_turns(): shard_in = lax.psum(shard_in, ii)  170 us
    ppermute x20, starting transfers between devices, extended(): lax.ppermute(head, axis, [((i + 1) % count, i) for i in range(ends)])  70.7 us
    ppermute x20, starting transfers between devices, extended(): lax.ppermute(tail, axis, [(i, (i + 1) % count) for i in range(ends)])  64.1 us
    ppermute x20, waiting for transfers between devices, extended(): lax.ppermute(head, axis, [((i + 1) % count, i) for i in range(ends)])  54.5 us
    ppermute x20, waiting for transfers between devices, extended(): lax.ppermute(tail, axis, [(i, (i + 1) % count) for i in range(ends)])  19.9 us
  transfers between devices with their start and end apart: 40, of which 25 were waited for; matrix products, arithmetic and copies ran while one was open for 2% of the time, Pallas kernels for 0%

profile of v1, /device:TPU:130, one launch (start us, length us, event | category | flops | bytes accessed | tf_op | source)
XLA Modules:
  0.0 450.8 jit_solution(10455792952849505930)
XLA Ops:
  3.7 4.9 %collective-permute-start.5 = (f32[2,16,1,128]{3,1,2,0:T(8,128)S(1)}, f32[2,16,1,128]{3,1,2,0:T(8,128)S(1)}, u32[]{:S(2)}, u32[]{:S(2)}) collective-permute-start(f32[2,16,1,128]{3,1,2,0:T(8,128)S(1)} %get-tuple-element.116), channel_id=1, source_target_pairs={{8,0},{16,8},{24,16},{32,24},{40,32},{48,40},{56,48},{64,56},{72,6... | collective-permute-start | bytes 49160 | tf_op jit(solution)/shard_map/ppermute | solution.py:27
  10.4 8.7 %all_gather.10 = f32[4,16,16,128]{3,2,1,0:T(8,128)S(1)} all-gather(f32[2,16,16,128]{3,2,1,0:T(8,128)S(1)} %broadcast_subtract_fusion), channel_id=1, replica_groups=mesh['section'=2,'sx'=16,'sy'=8] {'section'}, dimensions={0}, use_global_device_ids=true | all-gather | bytes 786432 | tf_op jit(solution)/shard_map/all_gather | solution.py:269
  25.8 4.9 %collective-permute-start.1 = (f32[4,16,1,128]{3,1,2,0:T(8,128)S(1)}, f32[4,16,1,128]{3,1,2,0:T(8,128)S(1)}, u32[]{:S(2)}, u32[]{:S(2)}) collective-permute-start(f32[4,16,1,128]{3,1,2,0:T(8,128)S(1)} %get-tuple-element.53), channel_id=1, source_target_pairs={{8,0},{16,8},{24,16},{32,24},{40,32},{48,40},{56,48},{64,56},{72,6... | collective-permute-start | bytes 98312 | tf_op jit(solution)/shard_map/ppermute | solution.py:27
  52.4 8.6 %all_gather.9 = f32[4,16,16,128]{3,2,1,0:T(8,128)S(1)} all-gather(f32[2,16,16,128]{3,2,1,0:T(8,128)S(1)} %copy.337), channel_id=1, replica_groups=mesh['section'=2,'sx'=16,'sy'=8] {'section'}, dimensions={0}, use_global_device_ids=true | all-gather | bytes 786432 | tf_op jit(solution)/shard_map/all_gather | solution.py:268
  65.5 4.9 %collective-permute-start.9 = (f32[2,16,1,128]{3,1,2,0:T(8,128)S(1)}, f32[2,16,1,128]{3,1,2,0:T(8,128)S(1)}, u32[]{:S(2)}, u32[]{:S(2)}) collective-permute-start(f32[2,16,1,128]{3,1,2,0:T(8,128)S(1)} %get-tuple-element.113), channel_id=1, source_target_pairs={{8,0},{16,8},{24,16},{32,24},{40,32},{48,40},{56,48},{64,56},{72,6... | collective-permute-start | bytes 49160 | tf_op jit(solution)/shard_map/ppermute | solution.py:27
  81.7 6.5 %collective-permute-done.11 = f32[2,16,18,1]{3,1,2,0:T(8,128)S(1)} collective-permute-done((f32[2,16,18,1]{3,1,2,0:T(8,128)S(1)}, f32[2,16,18,1]{3,1,2,0:T(8,128)S(1)}, u32[]{:S(2)}, u32[]{:S(2)}) %collective-permute-start.11) | collective-permute-done | bytes 2336 | tf_op jit(solution)/shard_map/ppermute | solution.py:27
  115.3 24.3 %all-reduce.13 = (f32[]{:T(128)}, f32[]{:T(128)}) all-reduce(f32[]{:T(128)} %get-tuple-element.12, f32[]{:T(128)} %get-tuple-element.11), channel_id=1, replica_groups=mesh['section'=2,'sx'=16,'sy'=8] {'sx'}, use_global_device_ids=true, to_apply=%region_1.2 | all-reduce | flops 2 | bytes 16 | tf_op jit(solution)/shard_map/psum | solution.py:13
  139.6 16.5 %all-reduce.17 = (f32[]{:T(128)}, f32[]{:T(128)}) all-reduce(f32[]{:T(128)} %get-tuple-element.19, f32[]{:T(128)} %get-tuple-element.20), channel_id=1, replica_groups=mesh['section'=2,'sx'=16,'sy'=8] {'sy'}, use_global_device_ids=true, to_apply=%region_2.3 | all-reduce | flops 2 | bytes 16 | tf_op jit(solution)/shard_map/psum | solution.py:13
  161.0 4.9 %collective-permute-start.17 = (f32[2,16,1,128]{3,1,2,0:T(8,128)S(1)}, f32[2,16,1,128]{3,1,2,0:T(8,128)S(1)}, u32[]{:S(2)}, u32[]{:S(2)}) collective-permute-start(f32[2,16,1,128]{3,1,2,0:T(8,128)S(1)} %get-tuple-element.109), channel_id=1, source_target_pairs={{8,0},{16,8},{24,16},{32,24},{40,32},{48,40},{56,48},{64,56},{72,6... | collective-permute-start | bytes 49160 | tf_op jit(solution)/shard_map/ppermute | solution.py:27
  190.1 6.1 %collective-permute-start.22 = (f32[2,16,18,1]{3,1,2,0:T(8,128)S(1)}, f32[2,16,18,1]{3,1,2,0:T(8,128)S(1)}, u32[]{:S(2)}, u32[]{:S(2)}) collective-permute-start(f32[2,16,18,1]{3,1,2,0:T(8,128)S(1)} %get-tuple-element.89), channel_id=1, source_target_pairs={{0,1},{1,2},{2,3},{3,4},{4,5},{5,6},{6,7},{8,9},{9,10},{10,11},{11... | collective-permute-start | bytes 6920 | tf_op jit(solution)/shard_map/ppermute | solution.py:25
  200.4 6.5 %collective-permute-done.23 = f32[2,16,18,1]{3,1,2,0:T(8,128)S(1)} collective-permute-done((f32[2,16,18,1]{3,1,2,0:T(8,128)S(1)}, f32[2,16,18,1]{3,1,2,0:T(8,128)S(1)}, u32[]{:S(2)}, u32[]{:S(2)}) %collective-permute-start.23) | collective-permute-done | bytes 2336 | tf_op jit(solution)/shard_map/ppermute | solution.py:27
  208.5 26.4 %all-reduce.12 = (f32[]{:T(128)}, f32[]{:T(128)}) all-reduce(f32[]{:T(128)} %get-tuple-element.10, f32[]{:T(128)} %get-tuple-element.9), channel_id=1, replica_groups=mesh['section'=2,'sx'=16,'sy'=8] {'sx'}, use_global_device_ids=true, to_apply=%region_7.8 | all-reduce | flops 2 | bytes 16 | tf_op jit(solution)/shard_map/psum | solution.py:13
  234.9 16.5 %all-reduce.16 = (f32[]{:T(128)}, f32[]{:T(128)}) all-reduce(f32[]{:T(128)} %get-tuple-element.17, f32[]{:T(128)} %get-tuple-element.18), channel_id=1, replica_groups=mesh['section'=2,'sx'=16,'sy'=8] {'sy'}, use_global_device_ids=true, to_apply=%region_8.9 | all-reduce | flops 2 | bytes 16 | tf_op jit(solution)/shard_map/psum | solution.py:13
  255.3 4.9 %collective-permute-start.25 = (f32[2,16,1,128]{3,1,2,0:T(8,128)S(1)}, f32[2,16,1,128]{3,1,2,0:T(8,128)S(1)}, u32[]{:S(2)}, u32[]{:S(2)}) collective-permute-start(f32[2,16,1,128]{3,1,2,0:T(8,128)S(1)} %get-tuple-element.105), channel_id=1, source_target_pairs={{8,0},{16,8},{24,16},{32,24},{40,32},{48,40},{56,48},{64,56},{72,6... | collective-permute-start | bytes 49160 | tf_op jit(solution)/shard_map/ppermute | solution.py:27
  277.8 4.9 %collective-permute-start.29 = (f32[2,16,1,128]{3,1,2,0:T(8,128)S(1)}, f32[2,16,1,128]{3,1,2,0:T(8,128)S(1)}, u32[]{:S(2)}, u32[]{:S(2)}) collective-permute-start(f32[2,16,1,128]{3,1,2,0:T(8,128)S(1)} %get-tuple-element.103), channel_id=1, source_target_pairs={{8,0},{16,8},{24,16},{32,24},{40,32},{48,40},{56,48},{64,56},{72,6... | collective-permute-start | bytes 49160 | tf_op jit(solution)/shard_map/ppermute | solution.py:27
  284.3 6.1 %collective-permute-start.30 = (f32[2,16,18,1]{3,1,2,0:T(8,128)S(1)}, f32[2,16,18,1]{3,1,2,0:T(8,128)S(1)}, u32[]{:S(2)}, u32[]{:S(2)}) collective-permute-start(f32[2,16,18,1]{3,1,2,0:T(8,128)S(1)} %get-tuple-element.85), channel_id=1, source_target_pairs={{0,1},{1,2},{2,3},{3,4},{4,5},{5,6},{6,7},{8,9},{9,10},{10,11},{11... | collective-permute-start | bytes 6920 | tf_op jit(solution)/shard_map/ppermute | solution.py:25
  294.7 6.5 %collective-permute-done.31 = f32[2,16,18,1]{3,1,2,0:T(8,128)S(1)} collective-permute-done((f32[2,16,18,1]{3,1,2,0:T(8,128)S(1)}, f32[2,16,18,1]{3,1,2,0:T(8,128)S(1)}, u32[]{:S(2)}, u32[]{:S(2)}) %collective-permute-start.31) | collective-permute-done | bytes 2336 | tf_op jit(solution)/shard_map/ppermute | solution.py:27
  302.7 26.4 %all-reduce.11 = (f32[]{:T(128)}, f32[]{:T(128)}) all-reduce(f32[]{:T(128)} %get-tuple-element.8, f32[]{:T(128)} %get-tuple-element.7), channel_id=1, replica_groups=mesh['section'=2,'sx'=16,'sy'=8] {'sx'}, use_global_device_ids=true, to_apply=%region_13.14 | all-reduce | flops 2 | bytes 16 | tf_op jit(solution)/shard_map/psum | solution.py:13
  329.1 16.5 %all-reduce.15 = (f32[]{:T(128)}, f32[]{:T(128)}) all-reduce(f32[]{:T(128)} %get-tuple-element.15, f32[]{:T(128)} %get-tuple-element.16), channel_id=1, replica_groups=mesh['section'=2,'sx'=16,'sy'=8] {'sy'}, use_global_device_ids=true, to_apply=%region_14.15 | all-reduce | flops 2 | bytes 16 | tf_op jit(solution)/shard_map/psum | solution.py:13
  378.5 6.1 %collective-permute-start.38 = (f32[2,16,18,1]{3,1,2,0:T(8,128)S(1)}, f32[2,16,18,1]{3,1,2,0:T(8,128)S(1)}, u32[]{:S(2)}, u32[]{:S(2)}) collective-permute-start(f32[2,16,18,1]{3,1,2,0:T(8,128)S(1)} %get-tuple-element.81), channel_id=1, source_target_pairs={{0,1},{1,2},{2,3},{3,4},{4,5},{5,6},{6,7},{8,9},{9,10},{10,11},{11... | collective-permute-start | bytes 6920 | tf_op jit(solution)/shard_map/ppermute | solution.py:25
  388.9 6.5 %collective-permute-done.39 = f32[2,16,18,1]{3,1,2,0:T(8,128)S(1)} collective-permute-done((f32[2,16,18,1]{3,1,2,0:T(8,128)S(1)}, f32[2,16,18,1]{3,1,2,0:T(8,128)S(1)}, u32[]{:S(2)}, u32[]{:S(2)}) %collective-permute-start.39) | collective-permute-done | bytes 2336 | tf_op jit(solution)/shard_map/ppermute | solution.py:27
  396.9 26.4 %all-reduce.10 = (f32[]{:T(128)}, f32[]{:T(128)}) all-reduce(f32[]{:T(128)} %get-tuple-element.6, f32[]{:T(128)} %get-tuple-element.5), channel_id=1, replica_groups=mesh['section'=2,'sx'=16,'sy'=8] {'sx'}, use_global_device_ids=true, to_apply=%region_19.20 | all-reduce | flops 2 | bytes 16 | tf_op jit(solution)/shard_map/psum | solution.py:13
  423.3 16.5 %all-reduce.14 = (f32[]{:T(128)}, f32[]{:T(128)}) all-reduce(f32[]{:T(128)} %get-tuple-element.13, f32[]{:T(128)} %get-tuple-element.14), channel_id=1, replica_groups=mesh['section'=2,'sx'=16,'sy'=8] {'sy'}, use_global_device_ids=true, to_apply=%region_20.21 | all-reduce | flops 2 | bytes 16 | tf_op jit(solution)/shard_map/psum | solution.py:13
  441.4 8.6 %all_gather.11 = f32[4,16,16,128]{3,2,1,0:T(8,128)S(1)} all-gather(f32[2,16,16,128]{3,2,1,0:T(8,128)S(1)} %copy.346), channel_id=1, replica_groups=mesh['section'=2,'sx'=16,'sy'=8] {'section'}, dimensions={0}, use_global_device_ids=true | all-gather | bytes 786432 | tf_op jit(solution)/shard_map/all_gather | solution.py:300
  (202 shorter events, 174.6 us)
Async XLA Ops:
  1.8 21.9 %collective-permute-start.4 = (f32[2,16,1,128]{3,1,2,0:T(8,128)S(1)}, f32[2,16,1,128]{3,1,2,0:T(8,128)S(1)}, u32[]{:S(2)}, u32[]{:S(2)}) collective-permute-start(f32[2,16,1,128]{3,1,2,0:T(8,128)S(1)} %get-tuple-element.117), channel_id=1, source_target_pairs={{0,8},{8,16},{16,24},{24,32},{32,40},{40,48},{48,56},{56,64},{64,7... | collective-permute-start | bytes 49160 | tf_op jit(solution)/shard_map/ppermute | solution.py:25
  3.7 27.0 %collective-permute-start.5 = (f32[2,16,1,128]{3,1,2,0:T(8,128)S(1)}, f32[2,16,1,128]{3,1,2,0:T(8,128)S(1)}, u32[]{:S(2)}, u32[]{:S(2)}) collective-permute-start(f32[2,16,1,128]{3,1,2,0:T(8,128)S(1)} %get-tuple-element.116), channel_id=1, source_target_pairs={{8,0},{16,8},{24,16},{32,24},{40,32},{48,40},{56,48},{64,56},{72,6... | collective-permute-start | bytes 49160 | tf_op jit(solution)/shard_map/ppermute | solution.py:27
  23.9 13.5 %collective-permute-start = (f32[4,16,1,128]{3,1,2,0:T(8,128)S(1)}, f32[4,16,1,128]{3,1,2,0:T(8,128)S(1)}, u32[]{:S(2)}, u32[]{:S(2)}) collective-permute-start(f32[4,16,1,128]{3,1,2,0:T(8,128)S(1)} %get-tuple-element.52), channel_id=1, source_target_pairs={{0,8},{8,16},{16,24},{24,32},{32,40},{40,48},{48,56},{56,64},{64,7... | collective-permute-start | bytes 98312 | tf_op jit(solution)/shard_map/ppermute | solution.py:25
  25.8 11.6 %collective-permute-start.1 = (f32[4,16,1,128]{3,1,2,0:T(8,128)S(1)}, f32[4,16,1,128]{3,1,2,0:T(8,128)S(1)}, u32[]{:S(2)}, u32[]{:S(2)}) collective-permute-start(f32[4,16,1,128]{3,1,2,0:T(8,128)S(1)} %get-tuple-element.53), channel_id=1, source_target_pairs={{8,0},{16,8},{24,16},{32,24},{40,32},{48,40},{56,48},{64,56},{72,6... | collective-permute-start | bytes 98312 | tf_op jit(solution)/shard_map/ppermute | solution.py:27
  30.9 13.7 %collective-permute-start.6 = (f32[2,16,18,1]{3,1,2,0:T(8,128)S(1)}, f32[2,16,18,1]{3,1,2,0:T(8,128)}, u32[]{:S(2)}, u32[]{:S(2)}) collective-permute-start(f32[2,16,18,1]{3,1,2,0:T(8,128)S(1)} %get-tuple-element.97), channel_id=1, source_target_pairs={{0,1},{1,2},{2,3},{3,4},{4,5},{5,6},{6,7},{8,9},{9,10},{10,11},{11... | collective-permute-start | bytes 6920 | tf_op jit(solution)/shard_map/ppermute | solution.py:25
  34.3 10.3 %collective-permute-start.7 = (f32[2,16,18,1]{3,1,2,0:T(8,128)S(1)}, f32[2,16,18,1]{3,1,2,0:T(8,128)}, u32[]{:S(2)}, u32[]{:S(2)}) collective-permute-start(f32[2,16,18,1]{3,1,2,0:T(8,128)S(1)} %get-tuple-element.96), channel_id=1, source_target_pairs={{1,0},{2,1},{3,2},{4,3},{5,4},{6,5},{7,6},{9,8},{10,9},{11,10},{12... | collective-permute-start | bytes 6920 | tf_op jit(solution)/shard_map/ppermute | solution.py:27
  38.2 7.8 %collective-permute-start.2 = (f32[4,16,18,1]{2,1,3,0:T(8,128)S(1)}, f32[4,16,18,1]{2,1,3,0:T(8,128)S(1)}, u32[]{:S(2)}, u32[]{:S(2)}) collective-permute-start(f32[4,16,18,1]{2,1,3,0:T(8,128)S(1)} %copy.321), channel_id=1, source_target_pairs={{0,1},{1,2},{2,3},{3,4},{4,5},{5,6},{6,7},{8,9},{9,10},{10,11},{11... | collective-permute-start | bytes 13832 | tf_op jit(solution)/shard_map/ppermute | solution.py:25
  71.9 9.8 %collective-permute-start.10 = (f32[2,16,18,1]{3,1,2,0:T(8,128)S(1)}, f32[2,16,18,1]{3,1,2,0:T(8,128)S(1)}, u32[]{:S(2)}, u32[]{:S(2)}) collective-permute-start(f32[2,16,18,1]{3,1,2,0:T(8,128)S(1)} %get-tuple-element.95), channel_id=1, source_target_pairs={{0,1},{1,2},{2,3},{3,4},{4,5},{5,6},{6,7},{8,9},{9,10},{10,11},{11... | collective-permute-start | bytes 6920 | tf_op jit(solution)/shard_map/ppermute | solution.py:25
  76.7 11.6 %collective-permute-start.11 = (f32[2,16,18,1]{3,1,2,0:T(8,128)S(1)}, f32[2,16,18,1]{3,1,2,0:T(8,128)S(1)}, u32[]{:S(2)}, u32[]{:S(2)}) collective-permute-start(f32[2,16,18,1]{3,1,2,0:T(8,128)S(1)} %get-tuple-element.94), channel_id=1, source_target_pairs={{1,0},{2,1},{3,2},{4,3},{5,4},{6,5},{7,6},{9,8},{10,9},{11,10},{12... | collective-permute-start | bytes 6920 | tf_op jit(solution)/shard_map/ppermute | solution.py:27
  98.2 10.4 %collective-permute-start.14 = (f32[2,16,18,1]{3,1,2,0:T(8,128)S(1)}, f32[2,16,18,1]{3,1,2,0:T(8,128)S(1)}, u32[]{:S(2)}, u32[]{:S(2)}) collective-permute-start(f32[2,16,18,1]{3,1,2,0:T(8,128)S(1)} %get-tuple-element.93), channel_id=1, source_target_pairs={{0,1},{1,2},{2,3},{3,4},{4,5},{5,6},{6,7},{8,9},{9,10},{10,11},{11... | collective-permute-start | bytes 6920 | tf_op jit(solution)/shard_map/ppermute | solution.py:25
  101.9 11.1 %collective-permute-start.15 = (f32[2,16,18,1]{3,1,2,0:T(8,128)S(1)}, f32[2,16,18,1]{3,1,2,0:T(8,128)S(1)}, u32[]{:S(2)}, u32[]{:S(2)}) collective-permute-start(f32[2,16,18,1]{3,1,2,0:T(8,128)S(1)} %get-tuple-element.92), channel_id=1, source_target_pairs={{1,0},{2,1},{3,2},{4,3},{5,4},{6,5},{7,6},{9,8},{10,9},{11,10},{12... | collective-permute-start | bytes 6920 | tf_op jit(solution)/shard_map/ppermute | solution.py:27
  167.5 8.6 %collective-permute-start.18 = (f32[2,16,18,1]{3,1,2,0:T(8,128)S(1)}, f32[2,16,18,1]{3,1,2,0:T(8,128)S(1)}, u32[]{:S(2)}, u32[]{:S(2)}) collective-permute-start(f32[2,16,18,1]{3,1,2,0:T(8,128)S(1)} %get-tuple-element.91), channel_id=1, source_target_pairs={{0,1},{1,2},{2,3},{3,4},{4,5},{5,6},{6,7},{8,9},{9,10},{10,11},{11... | collective-permute-start | bytes 6920 | tf_op jit(solution)/shard_map/ppermute | solution.py:25
  171.5 8.6 %collective-permute-start.19 = (f32[2,16,18,1]{3,1,2,0:T(8,128)S(1)}, f32[2,16,18,1]{3,1,2,0:T(8,128)S(1)}, u32[]{:S(2)}, u32[]{:S(2)}) collective-permute-start(f32[2,16,18,1]{3,1,2,0:T(8,128)S(1)} %get-tuple-element.90), channel_id=1, source_target_pairs={{1,0},{2,1},{3,2},{4,3},{5,4},{6,5},{7,6},{9,8},{10,9},{11,10},{12... | collective-permute-start | bytes 6920 | tf_op jit(solution)/shard_map/ppermute | solution.py:27
  190.1 10.4 %collective-permute-start.22 = (f32[2,16,18,1]{3,1,2,0:T(8,128)S(1)}, f32[2,16,18,1]{3,1,2,0:T(8,128)S(1)}, u32[]{:S(2)}, u32[]{:S(2)}) collective-permute-start(f32[2,16,18,1]{3,1,2,0:T(8,128)S(1)} %get-tuple-element.89), channel_id=1, source_target_pairs={{0,1},{1,2},{2,3},{3,4},{4,5},{5,6},{6,7},{8,9},{9,10},{10,11},{11... | collective-permute-start | bytes 6920 | tf_op jit(solution)/shard_map/ppermute | solution.py:25
  196.2 10.7 %collective-permute-start.23 = (f32[2,16,18,1]{3,1,2,0:T(8,128)S(1)}, f32[2,16,18,1]{3,1,2,0:T(8,128)S(1)}, u32[]{:S(2)}, u32[]{:S(2)}) collective-permute-start(f32[2,16,18,1]{3,1,2,0:T(8,128)S(1)} %get-tuple-element.88), channel_id=1, source_target_pairs={{1,0},{2,1},{3,2},{4,3},{5,4},{6,5},{7,6},{9,8},{10,9},{11,10},{12... | collective-permute-start | bytes 6920 | tf_op jit(solution)/shard_map/ppermute | solution.py:27
  261.7 8.6 %collective-permute-start.26 = (f32[2,16,18,1]{3,1,2,0:T(8,128)S(1)}, f32[2,16,18,1]{3,1,2,0:T(8,128)S(1)}, u32[]{:S(2)}, u32[]{:S(2)}) collective-permute-start(f32[2,16,18,1]{3,1,2,0:T(8,128)S(1)} %get-tuple-element.87), channel_id=1, source_target_pairs={{0,1},{1,2},{2,3},{3,4},{4,5},{5,6},{6,7},{8,9},{9,10},{10,11},{11... | collective-permute-start | bytes 6920 | tf_op jit(solution)/shard_map/ppermute | solution.py:25
  265.8 8.6 %collective-permute-start.27 = (f32[2,16,18,1]{3,1,2,0:T(8,128)S(1)}, f32[2,16,18,1]{3,1,2,0:T(8,128)S(1)}, u32[]{:S(2)}, u32[]{:S(2)}) collective-permute-start(f32[2,16,18,1]{3,1,2,0:T(8,128)S(1)} %get-tuple-element.86), channel_id=1, source_target_pairs={{1,0},{2,1},{3,2},{4,3},{5,4},{6,5},{7,6},{9,8},{10,9},{11,10},{12... | collective-permute-start | bytes 6920 | tf_op jit(solution)/shard_map/ppermute | solution.py:27
  284.3 10.4 %collective-permute-start.30 = (f32[2,16,18,1]{3,1,2,0:T(8,128)S(1)}, f32[2,16,18,1]{3,1,2,0:T(8,128)S(1)}, u32[]{:S(2)}, u32[]{:S(2)}) collective-permute-start(f32[2,16,18,1]{3,1,2,0:T(8,128)S(1)} %get-tuple-element.85), channel_id=1, source_target_pairs={{0,1},{1,2},{2,3},{3,4},{4,5},{5,6},{6,7},{8,9},{9,10},{10,11},{11... | collective-permute-start | bytes 6920 | tf_op jit(solution)/shard_map/ppermute | solution.py:25
  290.4 10.7 %collective-permute-start.31 = (f32[2,16,18,1]{3,1,2,0:T(8,128)S(1)}, f32[2,16,18,1]{3,1,2,0:T(8,128)S(1)}, u32[]{:S(2)}, u32[]{:S(2)}) collective-permute-start(f32[2,16,18,1]{3,1,2,0:T(8,128)S(1)} %get-tuple-element.84), channel_id=1, source_target_pairs={{1,0},{2,1},{3,2},{4,3},{5,4},{6,5},{7,6},{9,8},{10,9},{11,10},{12... | collective-permute-start | bytes 6920 | tf_op jit(solution)/shard_map/ppermute | solution.py:27
  355.9 8.6 %collective-permute-start.34 = (f32[2,16,18,1]{3,1,2,0:T(8,128)S(1)}, f32[2,16,18,1]{3,1,2,0:T(8,128)S(1)}, u32[]{:S(2)}, u32[]{:S(2)}) collective-permute-start(f32[2,16,18,1]{3,1,2,0:T(8,128)S(1)} %get-tuple-element.83), channel_id=1, source_target_pairs={{0,1},{1,2},{2,3},{3,4},{4,5},{5,6},{6,7},{8,9},{9,10},{10,11},{11... | collective-permute-start | bytes 6920 | tf_op jit(solution)/shard_map/ppermute | solution.py:25
  360.0 8.6 %collective-permute-start.35 = (f32[2,16,18,1]{3,1,2,0:T(8,128)S(1)}, f32[2,16,18,1]{3,1,2,0:T(8,128)S(1)}, u32[]{:S(2)}, u32[]{:S(2)}) collective-permute-start(f32[2,16,18,1]{3,1,2,0:T(8,128)S(1)} %get-tuple-element.82), channel_id=1, source_target_pairs={{1,0},{2,1},{3,2},{4,3},{5,4},{6,5},{7,6},{9,8},{10,9},{11,10},{12... | collective-permute-start | bytes 6920 | tf_op jit(solution)/shard_map/ppermute | solution.py:27
  370.1 6.8 %collective-permute-start.36 = (f32[2,16,1,128]{3,1,2,0:T(8,128)S(1)}, f32[2,16,1,128]{3,1,2,0:T(8,128)S(1)}, u32[]{:S(2)}, u32[]{:S(2)}) collective-permute-start(f32[2,16,1,128]{3,1,2,0:T(8,128)S(1)} %get-tuple-element.98), channel_id=1, source_target_pairs={{0,8},{8,16},{16,24},{24,32},{32,40},{40,48},{48,56},{56,64},{64,7... | collective-permute-start | bytes 49160 | tf_op jit(solution)/shard_map/ppermute | solution.py:25
  378.5 10.4 %collective-permute-start.38 = (f32[2,16,18,1]{3,1,2,0:T(8,128)S(1)}, f32[2,16,18,1]{3,1,2,0:T(8,128)S(1)}, u32[]{:S(2)}, u32[]{:S(2)}) collective-permute-start(f32[2,16,18,1]{3,1,2,0:T(8,128)S(1)} %get-tuple-element.81), channel_id=1, source_target_pairs={{0,1},{1,2},{2,3},{3,4},{4,5},{5,6},{6,7},{8,9},{9,10},{10,11},{11... | collective-permute-start | bytes 6920 | tf_op jit(solution)/shard_map/ppermute | solution.py:25
  384.7 10.7 %collective-permute-start.39 = (f32[2,16,18,1]{3,1,2,0:T(8,128)S(1)}, f32[2,16,18,1]{3,1,2,0:T(8,128)S(1)}, u32[]{:S(2)}, u32[]{:S(2)}) collective-permute-start(f32[2,16,18,1]{3,1,2,0:T(8,128)S(1)} %get-tuple-element.80), channel_id=1, source_target_pairs={{1,0},{2,1},{3,2},{4,3},{5,4},{6,5},{7,6},{9,8},{10,9},{11,10},{12... | collective-permute-start | bytes 6920 | tf_op jit(solution)/shard_map/ppermute | solution.py:27
  (33 other events, 355.5 us)
